TPU v7x, 32 devices: a whole 2x2x4 slice. The times are simulated.
32 devices in a mesh: section: 2 (over x), dp: 16 (over z, y, core).
Axes of the slice: x: 2, y: 2, z: 4, core: 2. Of those that a mesh axis runs over, the one named last changes fastest.
Arguments:
- inputs_long: bfloat16 [2, 16, 640, 768], P('section', 'dp'), may hold values from -6 to 6
- inputs_short: bfloat16 [2, 16, 256, 768], P('section', 'dp'), may hold values from -6 to 6
- cotangent_long: bfloat16 [2, 16, 640, 768], P('section', 'dp'), may hold values from -6 to 6
- cotangent_short: bfloat16 [2, 16, 256, 768], P('section', 'dp'), may hold values from -6 to 6
- lengths_long: int32 [2, 16], P(None, 'dp'), may hold values from 1 to 640, 7680 in all within a row
- lengths_short: int32 [2, 16], P(None, 'dp'), may hold values from 1 to 256, 3072 in all within a row
- self_in_weight: bfloat16 [2, 768, 2304], P('section'), may hold values from -0.3125 to 0.3125
- self_out_weight: bfloat16 [2, 768, 768], P('section'), may hold values from -0.625 to 0.625
- expand_weight: bfloat16 [2, 768, 3072], P('section'), may hold values from -0.21875 to 0.21875
- contract_weight: bfloat16 [2, 3072, 768], P('section'), may hold values from -0.109375 to 0.109375
- expand_bias: float32 [2, 3072], P('section'), may hold values from -1.75 to 1.75
- layer_biases: float32 [2, 6, 768], P('section'), may hold values from -1.75 to 1.75
- layer_gains: float32 [2, 2, 768], P('section'), may hold values from 0.25 to 1.75
- cross_weight: bfloat16 [768, 3072], replicated, may hold values from -0.3125 to 0.3125
- cross_biases: float32 [4, 768], replicated, may hold values from -1.75 to 1.75
- cross_gain: float32 [768], replicated, may hold values from 0.25 to 1.75
Outputs:
- outputs_long: bfloat16 [2, 16, 640, 768], P('section', 'dp')
- outputs_short: bfloat16 [2, 16, 256, 768], P('section', 'dp')
- input_grad_long: float32 [2, 16, 640, 768], P('section', 'dp')
- input_grad_short: float32 [2, 16, 256, 768], P('section', 'dp')
- self_in_grad: float32 [2, 768, 2304], P('section', 'dp')
- self_out_grad: float32 [2, 768, 768], P('section', 'dp')
- expand_grad: float32 [2, 768, 3072], P('section', 'dp')
- contract_grad: float32 [2, 3072, 768], P('section', 'dp')
- expand_bias_grad: float32 [2, 3072], P('section', 'dp')
- bias_grad: float32 [2, 6, 768], P('section', None, 'dp')
- gain_grad: float32 [2, 2, 768], P('section', None, 'dp')
- cross_grad: float32 [768, 3072], P(None, ('section', 'dp'))
- cross_bias_grad: float32 [4, 768], replicated
- cross_gain_grad: float32 [768], replicated
Inputs may be any that keep to these rules, and one draw needn't show every extreme that they name: In each row of lengths_long the lengths sum to 7680 and the largest is 640. In each row of lengths_short the lengths sum to 3072 and the largest is 256.
All inputs are finite; a program needn't handle non-finite values. No bound on the sum of `lengths_long` or of `lengths_short` on one device may be relied on, other than what follows from the above.
Results may differ from a plain program's by a relative error of at most 0.02.
Values may be sent and summed in bfloat16 or wider, within the bound.
A program may use at most 320 MiB of HBM per device.

v0:
```python
import jax
import jax.numpy as jnp
from jax import lax
from jax.sharding import PartitionSpec as P

HEAD_DIM = 64


EPSILON = 1e-05
MASKED = -1e30


def shifted(value, axis, steps):
    count = lax.axis_size(axis)
    leading, last = (max(0, -steps), min(count, count - steps))
    return lax.ppermute(value, axis, [(source, source + steps) for source in range(leading, last)])


def matmul(operand, factor):
    return jnp.dot(operand, factor, preferred_element_type=jnp.float32)


def transposed_times(operand, factor):
    return lax.dot_general(
        operand, factor, (((0,), (0,)), ((), ())), preferred_element_type=jnp.float32
    )


def times_transposed(operand, factor):
    return lax.dot_general(
        operand, factor, (((1,), (1,)), ((), ())), preferred_element_type=jnp.float32
    )


def rounded(value):
    return value.astype(jnp.bfloat16)


def column_sum(value):
    return jnp.sum(value.astype(jnp.float32), axis=0)


def layer_norm(hidden, gain, shift):
    centred = hidden - jnp.mean(hidden, axis=-1, keepdims=True)
    spread = jnp.mean(centred * centred, axis=-1, keepdims=True)
    return centred * lax.rsqrt(spread + EPSILON) * gain + shift


def gaussian_unit(value):
    return jax.nn.gelu(value, approximate=False)


def block_size(seq_length):
    return seq_length if seq_length <= 1024 else 512


def bucket_views(packed, buckets):
    pieces = []
    offset = 0
    for row_count, seq_length in buckets:
        amount = row_count * seq_length
        pieces.append(packed[offset : offset + amount].reshape(row_count, seq_length, -1, HEAD_DIM))
        offset += amount
    return pieces


def join_views(pieces):
    return jnp.concatenate(
        [piece.reshape(-1, piece.shape[2] * piece.shape[3]) for piece in pieces], 0
    )


def masked_scores(queries, key_rows, key_lengths, first_row, causal):
    scores = jnp.einsum(
        "bqhe,bkhe->bhqk", queries, key_rows, preferred_element_type=jnp.float32
    ) * HEAD_DIM ** (-0.5)
    key_place = jnp.arange(key_rows.shape[1])
    query_place = first_row + jnp.arange(queries.shape[1])
    allowed = key_place[None, None, :] < key_lengths[:, None, None]
    ordered = key_place[None, None, :] <= query_place[None, :, None]
    allowed = allowed & (ordered | jnp.logical_not(causal))
    return jnp.where(allowed[:, None], scores, MASKED)


def attend_forward(queries, key_rows, value_rows, key_lengths, causal):
    seq_length = queries.shape[1]
    block_rows = block_size(seq_length)
    results, totals = ([], [])
    for first_row in range(0, seq_length, block_rows):
        window = queries[:, first_row : first_row + block_rows]
        scores = masked_scores(window, key_rows, key_lengths, first_row, causal)
        highest = jnp.max(scores, axis=-1, keepdims=True)
        weights = jnp.exp(scores - highest)
        summed = jnp.sum(weights, axis=-1, keepdims=True)
        probability = rounded(weights / summed)
        results.append(
            jnp.einsum(
                "bhqk,bkhe->bqhe", probability, value_rows, preferred_element_type=jnp.float32
            )
        )
        totals.append(highest[..., 0] + jnp.log(summed[..., 0]))
    return (jnp.concatenate(results, 1), jnp.concatenate(totals, 2))


def attend_backward(queries, key_rows, value_rows, key_lengths, causal, log_totals, grad_out):
    seq_length = queries.shape[1]
    block_rows = block_size(seq_length)
    scale = HEAD_DIM ** (-0.5)
    grad_queries = []
    grad_keys = jnp.zeros(key_rows.shape, jnp.float32)
    grad_values = jnp.zeros(value_rows.shape, jnp.float32)
    for first_row in range(0, seq_length, block_rows):
        window = queries[:, first_row : first_row + block_rows]
        grad_window = grad_out[:, first_row : first_row + block_rows]
        scores = masked_scores(window, key_rows, key_lengths, first_row, causal)
        probability = jnp.exp(scores - log_totals[:, :, first_row : first_row + block_rows, None])
        grad_values = grad_values + jnp.einsum(
            "bhqk,bqhe->bkhe", rounded(probability), grad_window, preferred_element_type=jnp.float32
        )
        grad_prob = jnp.einsum(
            "bqhe,bkhe->bhqk", grad_window, value_rows, preferred_element_type=jnp.float32
        )
        row_inner = jnp.sum(probability * grad_prob, axis=-1, keepdims=True)
        grad_scores = rounded(probability * (grad_prob - row_inner))
        grad_queries.append(
            jnp.einsum("bhqk,bkhe->bqhe", grad_scores, key_rows, preferred_element_type=jnp.float32)
            * scale
        )
        grad_keys = (
            grad_keys
            + jnp.einsum("bhqk,bqhe->bkhe", grad_scores, window, preferred_element_type=jnp.float32)
            * scale
        )
    return (jnp.concatenate(grad_queries, 1), grad_keys, grad_values)


def attend_all(queries, key_rows, value_rows, key_lengths, causal, buckets):
    results, totals = ([], [])
    for query_part, key_part, value_part, length_part in zip(
        bucket_views(queries, buckets),
        bucket_views(key_rows, buckets),
        bucket_views(value_rows, buckets),
        key_lengths,
    ):
        output, log_total = attend_forward(query_part, key_part, value_part, length_part, causal)
        results.append(output)
        totals.append(log_total)
    return (join_views(results), totals)


def attend_all_back(queries, key_rows, value_rows, key_lengths, causal, buckets, totals, grad_out):
    gradient_lists = ([], [], [])
    for query_part, key_part, value_part, length_part, total_part, grad_part in zip(
        bucket_views(queries, buckets),
        bucket_views(key_rows, buckets),
        bucket_views(value_rows, buckets),
        key_lengths,
        totals,
        bucket_views(grad_out, buckets),
    ):
        part_grads = attend_backward(
            query_part, key_part, value_part, length_part, causal, total_part, grad_part
        )
        for collect, element in zip(gradient_lists, part_grads):
            collect.append(element)
    return (
        join_views(gradient_lists[0]),
        join_views(gradient_lists[1]),
        join_views(gradient_lists[2]),
    )


def self_project(tokens, in_weight, bias_rows):
    model_width = tokens.shape[1]
    joint = matmul(tokens, in_weight)
    queries = rounded(joint[:, :model_width] + bias_rows[0])
    key_rows = rounded(joint[:, model_width : 2 * model_width])
    value_rows = rounded(joint[:, 2 * model_width :] + bias_rows[1])
    return (queries, key_rows, value_rows)


def self_forward(tokens, weights, own_lengths, causal, buckets):
    in_weight, out_weight, bias_rows, gain_rows = weights
    queries, key_rows, value_rows = self_project(tokens, in_weight, bias_rows)
    attended, totals = attend_all(queries, key_rows, value_rows, own_lengths, causal, buckets)
    mixed = rounded(attended)
    hidden = tokens.astype(jnp.float32) + matmul(mixed, out_weight) + bias_rows[2]
    return (layer_norm(hidden, gain_rows[0], bias_rows[3]), mixed, totals)


def self_backward(tokens, weights, own_lengths, causal, buckets, mixed, totals, grad_norm):
    in_weight, out_weight, bias_rows, gain_rows = weights
    model_width = tokens.shape[1]
    queries, key_rows, value_rows = self_project(tokens, in_weight, bias_rows)
    hidden = tokens.astype(jnp.float32) + matmul(mixed, out_weight) + bias_rows[2]
    _, norm_back = jax.vjp(layer_norm, hidden, gain_rows[0], bias_rows[3])
    grad_hidden, grad_gain, grad_shift = norm_back(grad_norm)
    grad_branch = rounded(grad_hidden)
    grad_out_weight = transposed_times(mixed, grad_branch)
    grad_mixed = rounded(times_transposed(grad_branch, out_weight))
    grad_queries, grad_keys, grad_values = attend_all_back(
        queries, key_rows, value_rows, own_lengths, causal, buckets, totals, grad_mixed
    )
    grad_joint = rounded(jnp.concatenate([grad_queries, grad_keys, grad_values], 1))
    grad_in_weight = transposed_times(tokens, grad_joint)
    grad_tokens = grad_hidden + times_transposed(grad_joint, in_weight)
    joint_sums = column_sum(grad_joint)
    bias_grads = (
        joint_sums[:model_width],
        joint_sums[2 * model_width :],
        column_sum(grad_branch),
        grad_shift,
    )
    return (grad_tokens, grad_in_weight, grad_out_weight, bias_grads, grad_gain)


def expand_forward(normed, weights):
    expand_matrix, contract_matrix, expand_shift, bias_rows, gain_rows = weights
    inner = matmul(rounded(normed), expand_matrix) + expand_shift
    active = rounded(gaussian_unit(inner))
    hidden = normed + matmul(active, contract_matrix) + bias_rows[4]
    return layer_norm(hidden, gain_rows[1], bias_rows[5])


def expand_backward(normed, weights, grad_norm):
    expand_matrix, contract_matrix, expand_shift, bias_rows, gain_rows = weights
    low_normed = rounded(normed)
    inner = matmul(low_normed, expand_matrix) + expand_shift
    active_value, unit_back = jax.vjp(gaussian_unit, inner)
    active = rounded(active_value)
    hidden = normed + matmul(active, contract_matrix) + bias_rows[4]
    _, norm_back = jax.vjp(layer_norm, hidden, gain_rows[1], bias_rows[5])
    grad_hidden, grad_gain, grad_shift = norm_back(grad_norm)
    grad_branch = rounded(grad_hidden)
    grad_contract = transposed_times(active, grad_branch)
    grad_active = times_transposed(grad_branch, contract_matrix)
    grad_inner = rounded(unit_back(grad_active)[0])
    grad_expand = transposed_times(low_normed, grad_inner)
    grad_normed = grad_hidden + times_transposed(grad_inner, expand_matrix)
    return (
        grad_normed,
        grad_expand,
        grad_contract,
        column_sum(grad_inner),
        column_sum(grad_branch),
        grad_shift,
        grad_gain,
    )


def memory_project(memory, cross):
    cross_matrix, cross_shift, cross_scale = cross
    model_width = memory.shape[1]
    key_rows = rounded(matmul(memory, cross_matrix[:, model_width : 2 * model_width]))
    value_rows = rounded(
        matmul(memory, cross_matrix[:, 2 * model_width : 3 * model_width]) + cross_shift[1]
    )
    return (key_rows, value_rows)


def memory_backward(memory, cross, grad_keys, grad_values):
    cross_matrix, cross_shift, cross_scale = cross
    model_width = memory.shape[1]
    grad_key_weight = transposed_times(memory, grad_keys)
    grad_value_weight = transposed_times(memory, grad_values)
    grad_memory = rounded(
        times_transposed(grad_keys, cross_matrix[:, model_width : 2 * model_width])
        + times_transposed(grad_values, cross_matrix[:, 2 * model_width : 3 * model_width])
    )
    return (grad_memory, grad_key_weight, grad_value_weight, column_sum(grad_values))


def cross_forward(normed, key_rows, value_rows, cross, source_lengths, buckets):
    cross_matrix, cross_shift, cross_scale = cross
    model_width = normed.shape[1]
    queries = rounded(matmul(rounded(normed), cross_matrix[:, :model_width]) + cross_shift[0])
    attended, totals = attend_all(queries, key_rows, value_rows, source_lengths, False, buckets)
    mixed = rounded(attended)
    hidden = normed + matmul(mixed, cross_matrix[:, 3 * model_width :]) + cross_shift[2]
    return (layer_norm(hidden, cross_scale, cross_shift[3]), mixed, totals)


def cross_backward(
    normed, key_rows, value_rows, cross, source_lengths, buckets, mixed, totals, grad_norm
):
    cross_matrix, cross_shift, cross_scale = cross
    model_width = normed.shape[1]
    low_normed = rounded(normed)
    queries = rounded(matmul(low_normed, cross_matrix[:, :model_width]) + cross_shift[0])
    hidden = normed + matmul(mixed, cross_matrix[:, 3 * model_width :]) + cross_shift[2]
    _, norm_back = jax.vjp(layer_norm, hidden, cross_scale, cross_shift[3])
    grad_hidden, grad_gain, grad_shift = norm_back(grad_norm)
    grad_branch = rounded(grad_hidden)
    grad_out_weight = transposed_times(mixed, grad_branch)
    grad_mixed = rounded(times_transposed(grad_branch, cross_matrix[:, 3 * model_width :]))
    grad_queries, grad_keys, grad_values = attend_all_back(
        queries, key_rows, value_rows, source_lengths, False, buckets, totals, grad_mixed
    )
    grad_queries = rounded(grad_queries)
    grad_query_weight = transposed_times(low_normed, grad_queries)
    grad_normed = grad_hidden + times_transposed(grad_queries, cross_matrix[:, :model_width])
    return (
        grad_normed,
        rounded(grad_keys),
        rounded(grad_values),
        grad_query_weight,
        grad_out_weight,
        column_sum(grad_queries),
        column_sum(grad_branch),
        grad_shift,
        grad_gain,
    )


def zero_expand(token_count, model_width, hidden_width):
    zero_row = jnp.zeros((model_width,), jnp.float32)
    return (
        jnp.zeros((token_count, model_width), jnp.float32),
        jnp.zeros((model_width, hidden_width), jnp.float32),
        jnp.zeros((hidden_width, model_width), jnp.float32),
        jnp.zeros((hidden_width,), jnp.float32),
        zero_row,
        zero_row,
        zero_row,
    )


def zero_cross(token_count, model_width):
    zero_row = jnp.zeros((model_width,), jnp.float32)
    zero_square = jnp.zeros((model_width, model_width), jnp.float32)
    zero_tokens = jnp.zeros((token_count, model_width), jnp.bfloat16)
    return (
        jnp.zeros((token_count, model_width), jnp.float32),
        zero_tokens,
        zero_tokens,
        zero_square,
        zero_square,
        zero_row,
        zero_row,
        zero_row,
        zero_row,
    )


def zero_memory(token_count, model_width):
    zero_square = jnp.zeros((model_width, model_width), jnp.float32)
    return (
        jnp.zeros((token_count, model_width), jnp.bfloat16),
        zero_square,
        zero_square,
        jnp.zeros((model_width,), jnp.float32),
    )


def shards(
    inputs_long,
    inputs_short,
    cotangent_long,
    cotangent_short,
    lengths_long,
    lengths_short,
    self_in_weight,
    self_out_weight,
    expand_weight,
    contract_weight,
    expand_bias,
    layer_biases,
    layer_gains,
    cross_weight,
    cross_biases,
    cross_gain,
):
    decoder = lax.axis_index("section") == 1
    model_width = inputs_long.shape[-1]
    hidden_width = expand_weight.shape[2]
    buckets = (
        (inputs_long.shape[1], inputs_long.shape[2]),
        (inputs_short.shape[1], inputs_short.shape[2]),
    )
    long_count = buckets[0][0] * buckets[0][1]
    tokens = jnp.concatenate(
        [inputs_long[0].reshape(-1, model_width), inputs_short[0].reshape(-1, model_width)], 0
    )
    token_count = tokens.shape[0]
    source_lengths = (lengths_long[0], lengths_short[0])
    own_lengths = (
        jnp.where(decoder, lengths_long[1], lengths_long[0]),
        jnp.where(decoder, lengths_short[1], lengths_short[0]),
    )
    self_weights = (self_in_weight[0], self_out_weight[0], layer_biases[0], layer_gains[0])
    expand_weights = (
        expand_weight[0],
        contract_weight[0],
        expand_bias[0],
        layer_biases[0],
        layer_gains[0],
    )
    cross = (cross_weight, cross_biases, cross_gain)
    empty = jnp.zeros((token_count, model_width), jnp.bfloat16)
    normed, self_mixed, self_totals = self_forward(
        tokens, self_weights, own_lengths, decoder, buckets
    )
    encoded = lax.cond(decoder, lambda: normed, lambda: expand_forward(normed, expand_weights))
    memory = rounded(encoded)
    received = shifted(memory, "section", 1)
    key_rows, value_rows = lax.cond(
        decoder, lambda: memory_project(received, cross), lambda: (empty, empty)
    )

    def decoder_forward():
        crossed_value, mixed_value, totals_value = cross_forward(
            normed, key_rows, value_rows, cross, source_lengths, buckets
        )
        return (
            expand_forward(crossed_value, expand_weights),
            crossed_value,
            mixed_value,
            totals_value,
        )

    def encoder_keep():
        return (encoded, normed, empty, [jnp.zeros_like(member) for member in self_totals])

    final, crossed, cross_mixed, cross_totals = lax.cond(decoder, decoder_forward, encoder_keep)
    out_tokens = rounded(final)
    outputs_long = out_tokens[:long_count].reshape(inputs_long.shape)
    outputs_short = out_tokens[long_count:].reshape(inputs_short.shape)

    def masked(cotangent, lengths):
        keep = jnp.arange(cotangent.shape[2])[None, :] < lengths[:, None]
        return jnp.where(keep[:, :, None], cotangent[0].astype(jnp.float32), 0.0).reshape(
            -1, model_width
        )

    grad_final = jnp.concatenate(
        [masked(cotangent_long, own_lengths[0]), masked(cotangent_short, own_lengths[1])], 0
    )

    def decoder_back():
        expand_value = expand_backward(crossed, expand_weights, grad_final)
        cross_value = cross_backward(
            normed,
            key_rows,
            value_rows,
            cross,
            source_lengths,
            buckets,
            cross_mixed,
            cross_totals,
            expand_value[0],
        )
        return (expand_value, cross_value)

    def encoder_wait():
        return (
            zero_expand(token_count, model_width, hidden_width),
            zero_cross(token_count, model_width),
        )

    expand_part, cross_part = lax.cond(decoder, decoder_back, encoder_wait)
    memory_part = lax.cond(
        decoder,
        lambda: memory_backward(received, cross, cross_part[1], cross_part[2]),
        lambda: zero_memory(token_count, model_width),
    )
    returned = shifted(memory_part[0], "section", -1)

    def encoder_back():
        return expand_backward(normed, expand_weights, grad_final + returned.astype(jnp.float32))

    expand_all = lax.cond(decoder, lambda: expand_part, encoder_back)
    grad_normed = jnp.where(decoder, cross_part[0], expand_all[0])
    grad_tokens, grad_in_weight, grad_out_weight, self_bias_grads, self_gain_grad = self_backward(
        tokens, self_weights, own_lengths, decoder, buckets, self_mixed, self_totals, grad_normed
    )
    input_grad_long = grad_tokens[:long_count].reshape(inputs_long.shape)
    input_grad_short = grad_tokens[long_count:].reshape(inputs_short.shape)
    bias_stack = jnp.stack(
        [
            self_bias_grads[0],
            self_bias_grads[1],
            self_bias_grads[2],
            self_bias_grads[3],
            expand_all[4],
            expand_all[5],
        ]
    )[None]
    gain_stack = jnp.stack([self_gain_grad, expand_all[6]])[None]
    cross_full = jnp.concatenate([cross_part[3], memory_part[1], memory_part[2], cross_part[4]], 1)
    cross_bias_full = jnp.stack([cross_part[5], memory_part[3], cross_part[6], cross_part[7]])
    summed = (
        lax.psum_scatter(grad_in_weight[None], "dp", scatter_dimension=1, tiled=True),
        lax.psum_scatter(grad_out_weight[None], "dp", scatter_dimension=1, tiled=True),
        lax.psum_scatter(expand_all[1][None], "dp", scatter_dimension=1, tiled=True),
        lax.psum_scatter(expand_all[2][None], "dp", scatter_dimension=1, tiled=True),
        lax.psum_scatter(expand_all[3][None], "dp", scatter_dimension=1, tiled=True),
        lax.psum_scatter(bias_stack, "dp", scatter_dimension=2, tiled=True),
        lax.psum_scatter(gain_stack, "dp", scatter_dimension=2, tiled=True),
    )
    cross_grad = lax.psum_scatter(cross_full, ("section", "dp"), scatter_dimension=1, tiled=True)
    cross_bias_grad, cross_gain_grad = lax.psum((cross_bias_full, cross_part[8]), ("section", "dp"))
    return (
        outputs_long,
        outputs_short,
        input_grad_long,
        input_grad_short,
        summed[0],
        summed[1],
        summed[2],
        summed[3],
        summed[4],
        summed[5],
        summed[6],
        cross_grad,
        cross_bias_grad,
        cross_gain_grad,
    )


def solution(mesh):
    in_specs = (
        P("section", "dp", None, None),
        P("section", "dp", None, None),
        P("section", "dp", None, None),
        P("section", "dp", None, None),
        P(None, "dp"),
        P(None, "dp"),
        P("section", None, None),
        P("section", None, None),
        P("section", None, None),
        P("section", None, None),
        P("section", None),
        P("section", None, None),
        P("section", None, None),
        P(),
        P(),
        P(),
    )
    out_specs = (
        P("section", "dp", None, None),
        P("section", "dp", None, None),
        P("section", "dp", None, None),
        P("section", "dp", None, None),
        P("section", "dp", None),
        P("section", "dp", None),
        P("section", "dp", None),
        P("section", "dp", None),
        P("section", "dp"),
        P("section", None, "dp"),
        P("section", None, "dp"),
        P(None, ("section", "dp")),
        P(),
        P(),
    )
    return jax.shard_map(shards, mesh=mesh, in_specs=in_specs, out_specs=out_specs, check_vma=False)
```

profile of v0, /device:TPU:0, one launch (start us, length us, event | category | flops | bytes accessed | tf_op | source)
XLA Modules:
  0.0 1420.8 jit_solution(85478455790623304)
XLA Ops:
  42.4 12.1 fusion.224
  54.5 9.8 fusion.162
  64.4 10.5 fusion.184
  96.4 46.5 %conditional.6 = (f32[896,768]{0,1:T(8,128)}) conditional(s32[]{:T(128)} %convert_element_type.199, (f32[896,768]{0,1:T(8,128)}, bf16[768,3072]{1,0:T(8,128)(2,1)}, f32[1,3072]{1,0:T(1,128)}, bf16[3072,768]{1,0:T(8,128)(2,1)}, f32[6,768]{1,0:T(8,128)}, /*index=5*/f32[2,768]{1,0:T(2,128)S(1)}) %tuple.195, f32[896,768]{0,1:T(8,128)} %get-tuple-element.533), branch_computations={%region_6.9_spmd, %region_9.10_spmd} | conditional | flops 8644953088 | bytes 34282020 | solution.py:403
  97.9 40.0 %fusion.209 = (f32[896]{0:T(1024)}, f32[896,768]{0,1:T(8,128)}) fusion(f32[768]{0:T(1024)} %get-tuple-element.433, f32[896,768]{0,1:T(8,128)} %get-tuple-element.140, bf16[3072,768]{1,0:T(8,128)(2,1)} %get-tuple-element.143, f32[3072]{0:T(1024)} %bitcast.385, bf16[768,3072]{1,0:T(8,128)(2,1)} %get-tuple-element.141), kind=kOutput, calls=%fused_computation.395 | convolution fusion | flops 8640134144 | bytes 14961152 | tf_op jit(solution)/shard_map/cond/branch_0_fun/dot_general | solution.py:20
  148.2 29.6 %collective-permute-done = bf16[896,768]{1,0:T(8,128)(2,1)} collective-permute-done((bf16[896,768]{1,0:T(8,128)(2,1)}, bf16[896,768]{1,0:T(8,128)(2,1)}, u32[]{:S(2)}, u32[]{:S(2)}) %collective-permute-start) | collective-permute-done | bytes 1376288 | tf_op jit(solution)/shard_map/ppermute | solution.py:16
  180.1 14.4 %conditional.8 = (f32[896,768]{0,1:T(8,128)}, f32[896,768]{0,1:T(8,128)}, bf16[896,768]{0,1:T(8,128)(2,1)}, f32[1,12,640]{2,1,0:T(8,128)S(1)}, f32[1,12,256]{2,1,0:T(8,128)S(1)}) conditional(s32[]{:T(128)} %convert_element_type.199, (f32[896,768]{0,1:T(8,128)}, f32[896,768]{0,1:T(8,128)}) %tuple.69, (s32[1,1]{1,0:T(1,128)}, f32[896,768]{0,1:T(8,128)}, ...), branch_computations={%region_12.13_spmd, %region_13.22_spmd} | conditional | flops 12299297792 | bytes 164884448 | solution.py:424
  195.1 26.6 %conditional.9 = (f32[896,768]{0,1:T(8,128)}, f32[768,3072]{0,1:T(8,128)}, f32[3072,768]{1,0:T(8,128)}, f32[3072]{0:T(1024)}, f32[768]{0:T(1024)}, /*index=5*/f3...) conditional(s32[]{:T(128)} %convert_element_type.199, () %tuple.73, ...), branch_computations={%region_22.23_spmd, %region_23.42_spmd} | conditional | flops 35727110144 | bytes 672250880 | solution.py:460
  233.7 321.6 %collective-permute-done.1 = bf16[896,768]{0,1:T(8,128)(2,1)S(1)} collective-permute-done((bf16[896,768]{0,1:T(8,128)(2,1)}, bf16[896,768]{0,1:T(8,128)(2,1)S(1)}, u32[]{:S(2)}, u32[]{:S(2)}) %collective-permute-start.1) | collective-permute-done | bytes 1376288 | tf_op jit(solution)/shard_map/ppermute | solution.py:16
  555.4 88.3 %conditional.11 = (f32[896,768]{0,1:T(8,128)}, f32[768,3072]{0,1:T(8,128)}, f32[3072,768]{1,0:T(8,128)}, f32[3072]{0:T(1024)}, f32[1,768]{1,0:T(1,128)S(1)}, /*index=5*/f32[1,768]{1,0:T(1,128)S(1)}, f32[1,768]{1,0:T(1,128)S(1)}) conditional(s32[]{:T(128)} %convert_element_type.199, (bf16[896,768]{0,1:T(8,128)(2,1)S(1)}, f32[896,768]{0,1:T(8,128)}, ...), branch_computations={%region_45.54_spmd, %region_54.55_spmd} | conditional | flops 25618317312 | bytes 237147936 | solution.py:471
  555.6 32.2 %multiply_convert_fusion.5 = (bf16[896,3072]{1,0:T(8,128)(2,1)}, f32[896,3072]{1,0:T(8,128)}, f32[896,3072]{1,0:T(8,128)}) fusion(f32[3072]{0:T(1024)} %bitcast.389, bf16[768,3072]{1,0:T(8,128)(2,1)} %get-tuple-element.190, f32[896,768]{0,1:T(8,128)} %get-tuple-element.189), kind=kOutput, calls=%fused_computation.260 | convolution fusion | flops 4410212352 | bytes 35008512 | tf_op jit(solution)/shard_map/cond/branch_0_fun/dot_general | solution.py:20
  609.7 15.1 %convert_reduce_fusion.5 = (f32[3072]{0:T(1024)}, bf16[896,3072]{1,0:T(8,128)(2,1)}) fusion(f32[896,3072]{1,0:T(8,128)} %get-tuple-element.478, f32[896,3072]{1,0:T(8,128)} %get-tuple-element.507, f32[3072]{0:T(1024)S(1)} %bitcast.390, bf16[896,768]{0,1:T(8,128)(2,1)S(1)} %get-tuple-element.472, bf16[3072,768]{1,0:T(8,128)(2,1)} %get-tuple-element.192), kind=kOutput, calls=%fused_computation.258 | convolution fusion | flops 4274648064 | bytes 33644544 | tf_op jit(solution)/shard_map/cond/branch_0_fun/dot_general | solution.py:30
  624.8 10.0 convolution_bitcast_fusion.3
  652.2 12.6 multiply_reduce_fusion.14
  664.8 13.6 multiply_convert_fusion.6
  689.6 10.9 fusion.185
  744.2 9.6 copy.172
  758.3 40.2 %all-reduce = (f32[4,768]{1,0:T(4,128)}, f32[768]{0:T(1024)}) all-reduce(f32[4,768]{1,0:T(4,128)S(1)} %pad_maximum_fusion.14, f32[768]{0:T(1024)} %get-tuple-element.282), channel_id=1, replica_groups=mesh['section'=2,'dp'=16] {'section','dp'}, use_global_device_ids=true, to_apply=%region_71.72 | all-reduce | flops 3840 | bytes 30720 | tf_op jit(solution)/shard_map/psum | solution.py:501
  824.1 56.9 %reduce-scatter.27.cloned.1.call-done = f32[48,6]{1,0:T(8,128)} async-done(((f32[768,6]{1,0:T(8,128)}), f32[48,6]{1,0:T(8,128)}) %reduce-scatter.27.cloned.1.call-update) | async-done | bytes 1168
  884.1 63.5 %reduce-scatter.17.cloned.1.call-done = f32[1,48,768]{2,1,0:T(8,128)} async-done(((f32[1,768,768]{2,1,0:T(8,128)}), f32[1,48,768]{2,1,0:T(8,128)}) %reduce-scatter.17.cloned.1.call-update) | async-done | bytes 147472 | tf_op jit(solution)/shard_map/reduce_scatter | solution.py:493
  947.7 93.4 %reduce-scatter.15.cloned.1.call-done = f32[1,48,2304]{2,1,0:T(8,128)} async-done(((f32[1,768,2304]{2,1,0:T(8,128)}), f32[1,48,2304]{2,1,0:T(8,128)}) %reduce-scatter.15.cloned.1.call-update) | async-done | bytes 442384 | tf_op jit(solution)/shard_map/reduce_scatter | solution.py:492
  1041.1 142.2 %reduce-scatter.23.cloned.1.call-done = f32[768,96]{0,1:T(8,128)} async-done(((f32[768,3072]{0,1:T(8,128)}), f32[768,96]{0,1:T(8,128)}) %reduce-scatter.23.cloned.1.call-update) | async-done | bytes 294928 | tf_op jit(solution)/shard_map/reduce_scatter | solution.py:500
  1183.3 114.8 %reduce-scatter.19.cloned.1.call-done = f32[1,48,3072]{2,1,0:T(8,128)} async-done(((f32[1,768,3072]{2,1,0:T(8,128)}), f32[1,48,3072]{2,1,0:T(8,128)}) %reduce-scatter.19.cloned.1.call-update) | async-done | bytes 589840 | tf_op jit(solution)/shard_map/reduce_scatter | solution.py:494
  1298.1 115.6 %reduce-scatter.21.cloned.1.call-done = f32[1,192,768]{2,1,0:T(8,128)} async-done(((f32[1,3072,768]{2,1,0:T(8,128)}), f32[1,192,768]{2,1,0:T(8,128)}) %reduce-scatter.21.cloned.1.call-update) | async-done | bytes 589840 | tf_op jit(solution)/shard_map/reduce_scatter | solution.py:495
  (277 shorter events, 240.4 us)
Async XLA Ops:
  7.2 812.4 %reduce-scatter.29.cloned.1.call-start = ((), (), s32[]{:S(2)}) async-start(), calls=%async_computation.15 | async-start | bytes 417792
  22.9 12.1 copy-start.90
  28.4 26.1 %copy-start.85 = (pred[640]{0:T(1024)(128)(4,1)}, pred[640]{0:T(1024)(128)(4,1)S(1)}, u32[]{:S(2)}) copy-start(pred[640]{0:T(1024)(128)(4,1)S(1)} %iota_compare_fusion.6) | copy-start | bytes 1924
  64.3 10.5 copy-start.26
  64.4 10.5 copy-start.46
  83.2 13.2 copy-start.54
  145.8 32.0 %collective-permute-start = (bf16[896,768]{1,0:T(8,128)(2,1)}, bf16[896,768]{1,0:T(8,128)(2,1)}, u32[]{:S(2)}, u32[]{:S(2)}) collective-permute-start(bf16[896,768]{1,0:T(8,128)(2,1)} %copy.153), channel_id=1, source_target_pairs={{0,16},{1,17},{2,18},{3,19},{4,20},{5,21},{6,22},{7,23},{8,24},{9,... | collective-permute-start | bytes 4128776 | tf_op jit(solution)/shard_map/ppermute | solution.py:16
  229.7 325.7 %collective-permute-start.1 = (bf16[896,768]{0,1:T(8,128)(2,1)}, bf16[896,768]{0,1:T(8,128)(2,1)S(1)}, u32[]{:S(2)}, u32[]{:S(2)}) collective-permute-start(bf16[896,768]{0,1:T(8,128)(2,1)} %copy.164), channel_id=1, source_target_pairs={{16,0},{17,1},{18,2},{19,3},{20,4},{21,5},{22,6},{23,7},{24,8},{25... | collective-permute-start | bytes 4128776 | tf_op jit(solution)/shard_map/ppermute | solution.py:16
  555.4 88.3 %copy-start.51 = (f32[896]{0:T(1024)S(1)}, f32[896]{0:T(1024)}, u32[]{:S(2)}) copy-start(f32[896]{0:T(1024)} %copy-done.50) | copy-start | bytes 10756
  555.4 88.4 %copy-start.53 = (f32[768]{0:T(1024)S(1)}, f32[768]{0:T(1024)}, u32[]{:S(2)}) copy-start(f32[768]{0:T(1024)} %copy-done.52) | copy-start | bytes 9220
  555.4 88.4 %copy-start.55 = (f32[896]{0:T(1024)S(1)}, f32[896]{0:T(1024)}, u32[]{:S(2)}) copy-start(f32[896]{0:T(1024)} %copy-done.54) | copy-start | bytes 10756
  555.5 32.2 %copy-start.66 = (f32[2,768]{1,0:T(2,128)S(1)}, f32[2,768]{1,0:T(2,128)}, u32[]{:S(2)}) copy-start(f32[2,768]{1,0:T(2,128)} %get-tuple-element.188) | copy-start | bytes 18436 | tf_op jit(solution)/shard_map/cond
  555.5 33.0 %copy-start.11 = (f32[896,768]{0,1:T(8,128)S(1)}, f32[896,768]{0,1:T(8,128)}, u32[]{:S(2)}) copy-start(f32[896,768]{0,1:T(8,128)} %get-tuple-element.189) | copy-start | bytes 8257540 | tf_op jit(solution)/shard_map/cond
  555.6 33.0 %copy-start.92 = (bf16[3072,768]{1,0:T(8,128)(2,1)S(1)}, bf16[3072,768]{1,0:T(8,128)(2,1)}, u32[]{:S(2)}) copy-start(bf16[3072,768]{1,0:T(8,128)(2,1)} %get-tuple-element.192) | copy-start | bytes 14155780 | tf_op jit(solution)/shard_map/cond
  664.8 13.6 copy-start.17
  689.6 12.3 copy-start.80
  703.0 119.6 %reduce-scatter.25.cloned.1.call-start = ((), (), s32[]{:S(2)}) async-start(), calls=%async_computation.13 | async-start | bytes 1671168
  718.1 162.9 %reduce-scatter.27.cloned.1.call-start = ((), (), s32[]{:S(2)}) async-start(), calls=%async_computation.14 | async-start | bytes 417792
  721.8 225.9 %reduce-scatter.17.cloned.1.call-start = ((), (), s32[]{:S(2)}) async-start(), calls=%async_computation.9 | async-start | bytes 2506752 | tf_op jit(solution)/shard_map/reduce_scatter | solution.py:493
  726.5 314.6 %reduce-scatter.15.cloned.1.call-start = ((), (), s32[]{:S(2)}) async-start(), calls=%async_computation.8 | async-start | bytes 7520256 | tf_op jit(solution)/shard_map/reduce_scatter | solution.py:492
  735.8 447.5 %reduce-scatter.23.cloned.1.call-start = ((), (), s32[]{:S(2)}) async-start(), calls=%async_computation.12 | async-start | bytes 9732096 | tf_op jit(solution)/shard_map/reduce_scatter | solution.py:500
  744.2 554.0 %reduce-scatter.19.cloned.1.call-start = ((), (), s32[]{:S(2)}) async-start(), calls=%async_computation.10 | async-start | bytes 10027008 | tf_op jit(solution)/shard_map/reduce_scatter | solution.py:494
  753.9 659.9 %reduce-scatter.21.cloned.1.call-start = ((), (), s32[]{:S(2)}) async-start(), calls=%async_computation.11 | async-start | bytes 10027008 | tf_op jit(solution)/shard_map/reduce_scatter | solution.py:495
  754.6 47.9 %copy-start.74 = (f32[896]{0:T(1024)S(1)}, f32[896]{0:T(1024)}, u32[]{:S(2)}) copy-start(f32[896]{0:T(1024)} %copy-done.73) | copy-start | bytes 10756
  (47 other events, 166.8 us)
Sparse Core Ops, SparseCore 0:
  703.1 56.4 reduce-scatter.28
  763.2 59.2 reduce-scatter.24
  826.0 54.9 reduce-scatter.26
  885.2 62.4 reduce-scatter.16
  952.1 88.9 reduce-scatter.14
  1047.4 135.8 reduce-scatter.22
  1188.0 110.0 reduce-scatter.18
  1302.8 110.8 reduce-scatter.20
where the time goes:
time: 1430 us; the launch traced here: 1420 us
  waiting for transfers between devices  940 us (66%)
  matrix products  209 us (15%)
  local copies, waits for them, and re-layouts  127 us (9%)
  other arithmetic  67.2 us (5%)
  blocking collectives  40.2 us (3%)
  between operations  17.7 us (1%)
  loops' own time  15.6 us (1%)
    ppermute x2, waiting for transfers between devices, shifted(): lax.ppermute(value, axis, [(source, source + steps) for source in range(l...  351 us
    reduce_scatter x1, waiting for transfers between devices, shards(): lax.psum_scatter(cross_full, ('section', 'dp'), scatter_dimension=1, tile...  142 us
    reduce_scatter x1, waiting for transfers between devices, shards(): lax.psum_scatter(expand_all[2][None], 'dp', scatter_dimension=1, tiled=True)  116 us
    reduce_scatter x1, waiting for transfers between devices, shards(): lax.psum_scatter(expand_all[1][None], 'dp', scatter_dimension=1, tiled=True)  115 us
    reduce_scatter x1, waiting for transfers between devices, shards(): lax.psum_scatter(grad_in_weight[None], 'dp', scatter_dimension=1, tiled=T...  93.4 us
    dot_general x5, matrix products, matmul(): return jnp.dot(operand, factor, preferred_element_type=jnp.float32)  86.8 us
    reduce_scatter x1, waiting for transfers between devices, shards(): lax.psum_scatter(grad_out_weight[None], 'dp', scatter_dimension=1, tiled=...  63.5 us
    unnamed x11, waiting for transfers between devices  59.3 us
  transfers between devices with their start and end apart: 10, of which 9 were waited for; matrix products, arithmetic and copies ran while one was open for 6% of the time, Pallas kernels for 0%

commit v1 on v0

v1 whole, which is shorter than its diff:
```python
import functools
import jax
import jax.numpy as jnp
from jax import lax
from jax.experimental import pallas as pl
from jax.experimental.pallas import tpu as pltpu
from jax.sharding import PartitionSpec as P

BF, F32 = jnp.bfloat16, jnp.float32
NEG = -1e30
NT = (((1,), (1,)), ((), ()))
TN = (((0,), (0,)), ((), ()))

def dot(a, b):
    return jnp.dot(a, b, preferred_element_type=F32)
def dot_nt(a, b):
    return lax.dot_general(a, b, NT, preferred_element_type=F32)
def dot_tn(a, b):
    return lax.dot_general(a, b, TN, preferred_element_type=F32)

def lanes(rows):
    return lax.broadcasted_iota(jnp.int32, (rows, 128), 1)

def split3(v):
    hi = v.astype(BF)
    rest = v - hi.astype(F32)
    mid = rest.astype(BF)
    low = (rest - mid.astype(F32)).astype(BF)
    return hi, mid, low

def norm_forward(u, gain, shift):
    mean = jnp.mean(u, axis=-1, keepdims=True)
    c = u - mean
    r = lax.rsqrt(jnp.mean(c * c, axis=-1, keepdims=True) + 1e-5)
    xhat = c * r
    return xhat, r, xhat * gain + shift

def attn_fwd_kernel(causal, same, len_ref, xq_ref, xkv_ref, res_ref, wqkv_ref, wo_ref, bias_ref, gain_ref,
                    qkv_ref, o_ref, lse_ref, xhat_ref, r_ref, n_ref):
    s, d = xq_ref.shape
    if not same:
        wo_ref = wqkv_ref.at[:, 3 * d :]
    xq = xq_ref[...].astype(BF)
    xkv = xq if same else xkv_ref[...]
    qkv_ref[:, :d] = (dot(xq, wqkv_ref[:, :d]) + bias_ref[0:1, :]).astype(BF)
    qkv_ref[:, d:2*d] = dot(xkv, wqkv_ref[:, d:2*d]).astype(BF)
    qkv_ref[:, 2*d:] = (dot(xkv, wqkv_ref[:, 2*d:3*d]) + bias_ref[1:2, :]).astype(BF)
    length = len_ref[0, 0]
    lane = lanes(s)
    row = lax.broadcasted_iota(jnp.int32, (s, 128), 0)
    key_bias = jnp.where(row < length, 0.0, NEG).astype(BF)
    if causal:
        tri = lax.broadcasted_iota(jnp.int32, (s, s), 1) <= lax.broadcasted_iota(jnp.int32, (s, s), 0)
    one = jnp.ones((s, 128), BF)
    zero = jnp.zeros((s, 128), BF)

    def pair(p, _):
        at = pl.multiple_of(p * 128, 128)
        q = qkv_ref[:, pl.ds(at, 128)] * jnp.asarray(0.125, BF)
        k = qkv_ref[:, pl.ds(d + at, 128)]
        v = qkv_ref[:, pl.ds(2 * d + at, 128)]
        outs, lses = [], []
        for h in range(2):
            mine = (lane < 64) if h == 0 else (lane >= 64)
            other = 64 if h == 0 else 0
            qh = jnp.where(mine, q, jnp.where(lane == other, one, zero))
            kh = jnp.where(mine, k, jnp.where(lane == other, key_bias, zero))
            sc = dot_nt(qh, kh)
            if causal:
                sc = jnp.where(tri, sc, NEG)
            m = jnp.max(sc, axis=-1, keepdims=True)
            e = jnp.exp(sc - m)
            l = jnp.sum(e, axis=-1, keepdims=True)
            outs.append(dot(e.astype(BF), v) * (1.0 / l))
            lses.append(m + jnp.log(l))
        o_ref[:, pl.ds(at, 128)] = jnp.where(lane < 64, outs[0], outs[1]).astype(BF)
        lse_ref[:, pl.ds(at, 128)] = jnp.where(lane < 64, lses[1], lses[0])
        return 0
    lax.fori_loop(0, d // 128, pair, 0)
    u = res_ref[...].astype(F32) + dot(o_ref[...], wo_ref[...]) + bias_ref[2:3, :]
    xhat, r, n = norm_forward(u, gain_ref[0:1, :], bias_ref[3:4, :])
    xhat_ref[...] = xhat
    r_ref[...] = jnp.broadcast_to(r, r_ref.shape)
    n_ref[...] = n

def attn_fwd(xq, xkv, res, wqkv, wo, bias, gain, length, causal):
    s, d = xq.shape
    same = xkv is None
    if same:
        xkv = xq
    else:
        wo = gain
    vm = pl.BlockSpec(memory_space=pltpu.VMEM)
    sm = pl.BlockSpec(memory_space=pltpu.SMEM)
    return pl.pallas_call(
        functools.partial(attn_fwd_kernel, causal, same),
        out_shape=(jax.ShapeDtypeStruct((s, 3 * d), BF), jax.ShapeDtypeStruct((s, d), BF), jax.ShapeDtypeStruct((s, d), F32),
                   jax.ShapeDtypeStruct((s, d), F32), jax.ShapeDtypeStruct((s, 128), F32), jax.ShapeDtypeStruct((s, d), F32)),
        in_specs=[sm] + [vm] * 7, out_specs=(vm,) * 6,
        compiler_params=pltpu.CompilerParams(vmem_limit_bytes=60 << 20),
    )(length.reshape(1, 1), xq, xkv, res, wqkv, wo, bias, gain)

def norm_backward(dn, xhat, r, gain):
    h = dn * gain
    return r * (h - jnp.mean(h, axis=-1, keepdims=True) - xhat * jnp.mean(h * xhat, axis=-1, keepdims=True))

def attn_bwd_kernel(causal, same, len_ref, dn_ref, qkv_ref, o_ref, lse_ref, xhat_ref, r_ref, wqkv_ref, wo_ref, gain_ref,
                    dres_ref, dqkv_ref, dt_ref, dkvx_ref, sums_ref, do_ref, dq_ref):
    s, d = dn_ref.shape
    if not same:
        wo_ref = wqkv_ref.at[:, 3 * d :]
    dn = dn_ref[...]
    xhat = xhat_ref[...]
    du = norm_backward(dn, xhat, r_ref[:, :1], gain_ref[0:1, :])
    dt = du.astype(BF)
    dt_ref[...] = dt
    sums_ref[2:3, :] = jnp.sum(dt.astype(F32), axis=0, keepdims=True)
    sums_ref[3:4, :] = jnp.sum(dn, axis=0, keepdims=True)
    sums_ref[4:5, :] = jnp.sum(dn * xhat, axis=0, keepdims=True)
    do_ref[...] = dot_nt(dt, wo_ref[...]).astype(BF)
    length = len_ref[0, 0]
    lane = lanes(s)
    row = lax.broadcasted_iota(jnp.int32, (s, 128), 0)
    key_bias = jnp.where(row < length, 0.0, NEG).astype(BF)
    if causal:
        tri = lax.broadcasted_iota(jnp.int32, (s, s), 0) <= lax.broadcasted_iota(jnp.int32, (s, s), 1)
    one = jnp.ones((s, 128), BF)
    zero = jnp.zeros((s, 128), BF)

    def place(base, mine, other, extra):
        out = zero
        for j, val in enumerate(extra):
            out = jnp.where(lane == other + j, val, out)
        return jnp.where(mine, base, out)

    def pair(p, _):
        at = pl.multiple_of(p * 128, 128)
        q = qkv_ref[:, pl.ds(at, 128)] * jnp.asarray(0.125, BF)
        k = qkv_ref[:, pl.ds(d + at, 128)]
        v = qkv_ref[:, pl.ds(2 * d + at, 128)]
        do = do_ref[:, pl.ds(at, 128)]
        lse3 = split3(-lse_ref[:, pl.ds(at, 128)])
        prod = do.astype(F32) * o_ref[:, pl.ds(at, 128)].astype(F32)
        dq, dk, dv = [], [], []
        for h in range(2):
            mine = (lane < 64) if h == 0 else (lane >= 64)
            other = 64 if h == 0 else 0
            inner = jnp.broadcast_to(jnp.sum(jnp.where(mine, prod, 0.0), axis=-1, keepdims=True), (s, 128))
            qh = place(q, mine, other, (*lse3, one))
            kh = place(k, mine, other, (one, one, one, key_bias))
            doh = place(do, mine, other, split3(-inner))
            vh = place(v, mine, other, (one, one, one))
            st = dot_nt(kh, qh)
            if causal:
                st = jnp.where(tri, st, NEG)
            pt = jnp.exp(st)
            dst = (pt * dot_nt(vh, doh)).astype(BF)
            dv.append(dot(pt.astype(BF), do))
            dk.append(dot(dst, q))
            dq.append(dot_tn(k, dst))
        m1 = lane < 64
        dq_ref[...] = jnp.where(lax.broadcasted_iota(jnp.int32, (128, s), 0) < 64, dq[0], dq[1])
        dqkv_ref[:, pl.ds(at, 128)] = (dq_ref[...].T * 0.125).astype(BF)
        dqkv_ref[:, pl.ds(d + at, 128)] = jnp.where(m1, dk[0], dk[1]).astype(BF)
        dqkv_ref[:, pl.ds(2 * d + at, 128)] = jnp.where(m1, dv[0], dv[1]).astype(BF)
        return 0
    lax.fori_loop(0, d // 128, pair, 0)
    if same:
        dres_ref[...] = du + dot_nt(dqkv_ref[...], wqkv_ref[...])
    else:
        dres_ref[...] = du + dot_nt(dqkv_ref[:, :d], wqkv_ref[:, :d])
        dkvx_ref[...] = dot_nt(dqkv_ref[:, d:], wqkv_ref[:, d:3*d]).astype(BF)
    sums_ref[0:1, :] = jnp.sum(dqkv_ref[:, :d].astype(F32), axis=0, keepdims=True)
    sums_ref[1:2, :] = jnp.sum(dqkv_ref[:, 2*d:].astype(F32), axis=0, keepdims=True)
    sums_ref[5:8, :] = jnp.zeros((3, d), F32)

def attn_bwd(dn, saved, wqkv, wo, gain, length, causal, same):
    qkv, o, lse, xhat, r = saved
    s, d = dn.shape
    if not same:
        wo = gain
    vm = pl.BlockSpec(memory_space=pltpu.VMEM)
    sm = pl.BlockSpec(memory_space=pltpu.SMEM)
    return pl.pallas_call(
        functools.partial(attn_bwd_kernel, causal, same),
        out_shape=(jax.ShapeDtypeStruct((s, d), F32), jax.ShapeDtypeStruct((s, 3 * d), BF), jax.ShapeDtypeStruct((s, d), BF),
                   jax.ShapeDtypeStruct((8, 128) if same else (s, d), BF), jax.ShapeDtypeStruct((8, d), F32)),
        in_specs=[sm] + [vm] * 9, out_specs=(vm,) * 5,
        scratch_shapes=[pltpu.VMEM((s, d), BF), pltpu.VMEM((128, s), F32)],
        compiler_params=pltpu.CompilerParams(vmem_limit_bytes=60 << 20),
    )(length.reshape(1, 1), dn, qkv, o, lse, xhat, r, wqkv, wo, gain)

def gelu_parts(a):
    e = jnp.exp(-0.5 * a * a)
    t = 1.0 / (1.0 + 0.23164188624 * jnp.abs(a))
    tail = t * (0.127414796 + t * (-0.142248368 + t * (0.7107068705 + t * (-0.7265760135 + t * 0.5307027145)))) * e
    phi_cap = jnp.where(a < 0.0, tail, 1.0 - tail)
    return phi_cap, e * 0.3989422804014327

def ffn_fwd_kernel(chunk, n_ref, we_ref, wc_ref, be_ref, bias_ref, gain_ref,
                   y_ref, g_ref, gp_ref, xhat_ref, r_ref, acc_ref):
    s, d = n_ref.shape
    ff = we_ref.shape[1]
    low = n_ref[...].astype(BF)
    acc_ref[...] = n_ref[...] + bias_ref[4:5, :]

    def step(c, _):
        at = pl.multiple_of(c * chunk, chunk)
        a = dot(low, we_ref[:, pl.ds(at, chunk)]) + be_ref[:, pl.ds(at, chunk)]
        cap, dens = gelu_parts(a)
        g = (a * cap).astype(BF)
        g_ref[:, pl.ds(at, chunk)] = g
        gp_ref[:, pl.ds(at, chunk)] = (cap + a * dens).astype(BF)
        acc_ref[...] += dot(g, wc_ref[pl.ds(at, chunk), :])
        return 0
    lax.fori_loop(0, ff // chunk, step, 0)
    xhat, r, y = norm_forward(acc_ref[...], gain_ref[1:2, :], bias_ref[5:6, :])
    xhat_ref[...] = xhat
    r_ref[...] = jnp.broadcast_to(r, r_ref.shape)
    y_ref[...] = y.astype(BF)

def ffn_fwd(n, we, wc, be, bias, gain, chunk=512):
    s, d = n.shape
    ff = we.shape[1]
    vm = pl.BlockSpec(memory_space=pltpu.VMEM)
    return pl.pallas_call(
        functools.partial(ffn_fwd_kernel, chunk),
        out_shape=(jax.ShapeDtypeStruct((s, d), BF), jax.ShapeDtypeStruct((s, ff), BF), jax.ShapeDtypeStruct((s, ff), BF),
                   jax.ShapeDtypeStruct((s, d), F32), jax.ShapeDtypeStruct((s, 128), F32)),
        in_specs=[vm] * 6, out_specs=(vm,) * 5,
        scratch_shapes=[pltpu.VMEM((s, d), F32)],
        compiler_params=pltpu.CompilerParams(vmem_limit_bytes=60 << 20),
    )(n, we, wc, be.reshape(1, ff), bias, gain)

def ffn_bwd_kernel(chunk, extra, len_ref, cot_ref, dm_ref, gp_ref, xhat_ref, r_ref, we_ref, wc_ref, gain_ref,
                   dn_ref, da_ref, dt_ref, sums_ref, sume_ref):
    s, d = cot_ref.shape
    ff = we_ref.shape[1]
    row = lax.broadcasted_iota(jnp.int32, (s, 1), 0)
    dy = jnp.where(row < len_ref[0, 0], cot_ref[...].astype(F32), 0.0)
    if extra:
        dy = dy + dm_ref[...].astype(F32)
    xhat = xhat_ref[...]
    du = norm_backward(dy, xhat, r_ref[:, :1], gain_ref[1:2, :])
    dt = du.astype(BF)
    dt_ref[...] = dt
    sums_ref[0:1, :] = jnp.sum(dt.astype(F32), axis=0, keepdims=True)
    sums_ref[1:2, :] = jnp.sum(dy, axis=0, keepdims=True)
    sums_ref[2:3, :] = jnp.sum(dy * xhat, axis=0, keepdims=True)
    sums_ref[3:8, :] = jnp.zeros((5, d), F32)
    dn_ref[...] = du

    def step(c, _):
        at = pl.multiple_of(c * chunk, chunk)
        dg = dot_nt(dt_ref[...], wc_ref[pl.ds(at, chunk), :])
        da = (dg * gp_ref[:, pl.ds(at, chunk)].astype(F32)).astype(BF)
        da_ref[:, pl.ds(at, chunk)] = da
        sume_ref[:, pl.ds(at, chunk)] = jnp.sum(da.astype(F32), axis=0, keepdims=True)
        dn_ref[...] += dot_nt(da, we_ref[:, pl.ds(at, chunk)])
        return 0
    lax.fori_loop(0, ff // chunk, step, 0)

def ffn_bwd(cot, dm, length, saved, we, wc, gain, chunk=512):
    gp, xhat, r = saved
    s, d = cot.shape
    ff = we.shape[1]
    extra = dm is not None
    vm = pl.BlockSpec(memory_space=pltpu.VMEM)
    sm = pl.BlockSpec(memory_space=pltpu.SMEM)
    return pl.pallas_call(
        functools.partial(ffn_bwd_kernel, chunk, extra),
        out_shape=(jax.ShapeDtypeStruct((s, d), F32), jax.ShapeDtypeStruct((s, ff), BF), jax.ShapeDtypeStruct((s, d), BF),
                   jax.ShapeDtypeStruct((8, d), F32), jax.ShapeDtypeStruct((1, ff), F32)),
        in_specs=[sm] + [vm] * 8, out_specs=(vm,) * 5,
        compiler_params=pltpu.CompilerParams(vmem_limit_bytes=60 << 20),
    )(length.reshape(1, 1), cot, dm if extra else cot, gp, xhat, r, we, wc, gain)

def wgrad_kernel(lengths, *refs):
    n = len(lengths)
    xs, dys, out_ref, xt_ref = refs[:n], refs[n:2*n], refs[2*n], refs[2*n+1]
    @pl.when(pl.program_id(0) == 0)
    def _():
        at = 0
        for x, s in zip(xs, lengths):
            xt_ref[:, at:at+s] = x[...].astype(BF).T
            at += s
    at, total = 0, None
    for dy, s in zip(dys, lengths):
        t = dot(xt_ref[:, at:at+s], dy[...].astype(BF))
        total = t if total is None else total + t
        at += s
    out_ref[...] = total.astype(BF)

def wgrad(xs, dys, tile=768):
    lengths = [x.shape[0] for x in xs]
    k, n = xs[0].shape[1], dys[0].shape[1]
    return pl.pallas_call(
        functools.partial(wgrad_kernel, lengths),
        out_shape=jax.ShapeDtypeStruct((k, n), BF),
        grid=(n // tile,),
        in_specs=[pl.BlockSpec((s, k), lambda i: (0, 0)) for s in lengths] + [pl.BlockSpec((s, tile), lambda i: (0, i)) for s in lengths],
        out_specs=pl.BlockSpec((k, tile), lambda i: (0, i)),
        scratch_shapes=[pltpu.VMEM((k, sum(lengths)), BF)],
        compiler_params=pltpu.CompilerParams(vmem_limit_bytes=60 << 20),
    )(*xs, *dys)


def small_rows(parts):
    total = parts[0]
    for part in parts[1:]:
        total = total + part
    return total


def shards(
    inputs_long,
    inputs_short,
    cotangent_long,
    cotangent_short,
    lengths_long,
    lengths_short,
    self_in_weight,
    self_out_weight,
    expand_weight,
    contract_weight,
    expand_bias,
    layer_biases,
    layer_gains,
    cross_weight,
    cross_biases,
    cross_gain,
):
    decoder = lax.axis_index("section") == 1
    d = inputs_long.shape[-1]
    ff = expand_weight.shape[2]
    w_in, w_out, w_e, w_c = self_in_weight[0], self_out_weight[0], expand_weight[0], contract_weight[0]
    b_e, bias, gain = expand_bias[0], layer_biases[0], layer_gains[0]
    c_gain = cross_gain.reshape(1, d)

    xs = (inputs_short[0, 0], inputs_long[0, 0])
    cots = (cotangent_short[0, 0], cotangent_long[0, 0])
    source = (lengths_short[0, 0], lengths_long[0, 0])
    target = (lengths_short[1, 0], lengths_long[1, 0])
    sizes = tuple(x.shape[0] for x in xs)

    def zeros_like_fwd(s):
        return (
            jnp.zeros((s, d), BF),
            jnp.zeros((s, ff), BF),
            jnp.zeros((s, ff), BF),
            jnp.zeros((s, d), F32),
            jnp.zeros((s, 128), F32),
        )

    def first(i):
        x = xs[i]

        def encode():
            out = attn_fwd(x, None, x, w_in, w_out, bias, gain, source[i], False)
            return out, ffn_fwd(out[5], w_e, w_c, b_e, bias, gain)

        def decode():
            out = attn_fwd(x, None, x, w_in, w_out, bias, gain, target[i], True)
            return out, zeros_like_fwd(sizes[i])

        return lax.cond(decoder, decode, encode)

    def send(value, steps):
        return lax.ppermute(value, "section", [(0, 1)] if steps > 0 else [(1, 0)])

    def middle(i, memory, n1):
        s = sizes[i]

        def decode():
            out = attn_fwd(n1, memory, n1, cross_weight, None, cross_biases, c_gain, source[i], False)
            y, g, gp, xhat, r = ffn_fwd(out[5], w_e, w_c, b_e, bias, gain)
            fb = ffn_bwd(cots[i], None, target[i], (gp, xhat, r), w_e, w_c, gain)
            ab = attn_bwd(fb[0], out[:5], cross_weight, None, c_gain, source[i], False, False)
            return (out[5], g, fb[1], fb[2], out[1], ab[1], ab[2]), ab[0], ab[3], y, (fb[3], fb[4], ab[4])

        def encode():
            return (
                (
                    jnp.zeros((s, d), F32),
                    jnp.zeros((s, ff), BF),
                    jnp.zeros((s, ff), BF),
                    jnp.zeros((s, d), BF),
                    jnp.zeros((s, d), BF),
                    jnp.zeros((s, 3 * d), BF),
                    jnp.zeros((s, d), BF),
                ),
                jnp.zeros((s, d), F32),
                jnp.zeros((s, d), BF),
                jnp.zeros((s, d), BF),
                (jnp.zeros((8, d), F32), jnp.zeros((1, ff), F32), jnp.zeros((8, d), F32)),
            )

        return lax.cond(decoder, decode, encode)

    def last(i, att, ffn, dn_dec, dm):
        s = sizes[i]

        def decode():
            ab = attn_bwd(dn_dec, att[:5], w_in, w_out, gain, target[i], True, True)
            return (
                (ab[0], ab[1], ab[2], ab[4]),
                (jnp.zeros((s, ff), BF), jnp.zeros((s, d), BF), jnp.zeros((8, d), F32), jnp.zeros((1, ff), F32)),
            )

        def encode():
            fb = ffn_bwd(cots[i], dm, source[i], ffn[2:], w_e, w_c, gain)
            ab = attn_bwd(fb[0], att[:5], w_in, w_out, gain, source[i], False, True)
            return (ab[0], ab[1], ab[2], ab[4]), fb[1:]

        return lax.cond(decoder, decode, encode)

    att0, ffn0 = first(0)
    mem0 = send(ffn0[0], 1)
    att1, ffn1 = first(1)
    mem1 = send(ffn1[0], 1)
    keep0, dn0, dm0, y0, sums0 = middle(0, mem0, att0[5])
    back0 = send(dm0, -1)
    keep1, dn1, dm1, y1, sums1 = middle(1, mem1, att1[5])
    back1 = send(dm1, -1)
    self0, enc0 = last(0, att0, ffn0, dn0, back0)
    self1, enc1 = last(1, att1, ffn1, dn1, back1)

    def cross_grads():
        low = (att0[5], att1[5])
        return jnp.concatenate(
            [
                wgrad((keep0[5][:, :d], keep1[5][:, :d]), low),
                wgrad((keep0[5][:, d:], keep1[5][:, d:]), (mem0, mem1)),
                wgrad((keep0[6], keep1[6]), (keep0[4], keep1[4])),
            ],
            0,
        )

    cross_full = lax.cond(decoder, cross_grads, lambda: jnp.zeros((4 * d, d), BF))

    def ffn_grads_dec():
        return (
            wgrad((keep0[0], keep1[0]), (keep0[2], keep1[2])),
            wgrad((keep0[1], keep1[1]), (keep0[3], keep1[3]), 256),
            sums0[0] + sums1[0],
            sums0[1] + sums1[1],
        )

    def ffn_grads_enc():
        return (
            wgrad((att0[5], att1[5]), (enc0[0], enc1[0])),
            wgrad((ffn0[1], ffn1[1]), (enc0[1], enc1[1]), 256),
            enc0[2] + enc1[2],
            enc0[3] + enc1[3],
        )

    g_expand, g_contract, ffn_sums, sum_e = lax.cond(decoder, ffn_grads_dec, ffn_grads_enc)
    g_in = wgrad(xs, (self0[1], self1[1]))
    g_out = wgrad((att0[1], att1[1]), (self0[2], self1[2]))
    self_sums = self0[3] + self1[3]
    cross_sums = sums0[2] + sums1[2]

    def scatter(value, dim):
        return lax.psum_scatter(value, "dp", scatter_dimension=dim, tiled=True)

    packed = scatter(jnp.concatenate([g_in, g_out, g_expand], 1), 0).astype(F32)
    contract = scatter(g_contract, 0).astype(F32)
    dp = lax.axis_size("dp")
    width = 4 * d // (2 * dp)
    halves = cross_full.reshape(2, dp, width, d).transpose(1, 0, 2, 3).reshape(4 * d, d)
    cross_mine = scatter(halves, 0)
    to_enc = send(cross_mine[:width], -1)
    cross_out = jnp.where(decoder, cross_mine[width:], to_enc).astype(F32).T

    rows = jnp.concatenate([self_sums[0:4], ffn_sums[0:2], self_sums[4:5], ffn_sums[2:3], sum_e.reshape(ff // d, d)], 0)
    blank = jnp.zeros_like(rows)
    every = jnp.concatenate([jnp.where(decoder, blank, rows), jnp.where(decoder, rows, blank), cross_sums[0:5]], 0)
    every = lax.psum(every, ("section", "dp"))
    count = rows.shape[0]
    own = jnp.where(decoder, every[count : 2 * count], every[:count])
    me = lax.axis_index("dp")
    cols = d // dp
    piece = lax.dynamic_slice_in_dim(own[:8], me * cols, cols, 1)
    e_piece = lax.dynamic_slice_in_dim(own[8:].reshape(1, ff), me * (ff // dp), ff // dp, 1)
    cross_vec = every[2 * count :]

    outs = [jnp.where(decoder, y, e)[None, None] for y, e in ((y0, ffn0[0]), (y1, ffn1[0]))]
    return (
        outs[1],
        outs[0],
        self1[0][None, None],
        self0[0][None, None],
        packed[None, :, : 3 * d],
        packed[None, :, 3 * d : 4 * d],
        packed[None, :, 4 * d :],
        contract[None],
        e_piece,
        piece[None, :6],
        piece[None, 6:8],
        cross_out,
        cross_vec[:4],
        cross_vec[4],
    )


def solution(mesh):
    in_specs = (
        P("section", "dp", None, None),
        P("section", "dp", None, None),
        P("section", "dp", None, None),
        P("section", "dp", None, None),
        P(None, "dp"),
        P(None, "dp"),
        P("section", None, None),
        P("section", None, None),
        P("section", None, None),
        P("section", None, None),
        P("section", None),
        P("section", None, None),
        P("section", None, None),
        P(),
        P(),
        P(),
    )
    out_specs = (
        P("section", "dp", None, None),
        P("section", "dp", None, None),
        P("section", "dp", None, None),
        P("section", "dp", None, None),
        P("section", "dp", None),
        P("section", "dp", None),
        P("section", "dp", None),
        P("section", "dp", None),
        P("section", "dp"),
        P("section", None, "dp"),
        P("section", None, "dp"),
        P(None, ("section", "dp")),
        P(),
        P(),
    )
    return jax.shard_map(shards, mesh=mesh, in_specs=in_specs, out_specs=out_specs, check_vma=False)
```

time: 1430 us -> 615 us (0.43)
  waiting for transfers between devices: 940 us -> 345 us
  matrix products: 209 us -> 0 us
  Pallas kernels: 0 us -> 161 us
  local copies, waits for them, and re-layouts: 127 us -> 48.1 us
  other arithmetic: 67.2 us -> 20.3 us
  blocking collectives: 40.2 us -> 0 us
    reduce_scatter x5 -> x3, waiting for transfers between devices: 530 us -> 122 us  [scatter(): return lax.psum_scatter(value, 'dp', scatter_dimension=dim, tiled=True)]
    ppermute x2 -> x5, waiting for transfers between devices: 351 us -> 110 us  [send(): return lax.ppermute(value, 'section', [(0, 1)] if steps > 0 else [(1, 0)])]
    dot_general x25 -> x0, matrix products: 209 us -> none  [the longest x5 86.8 us: matmul(): return jnp.dot(operand, factor, preferred_element_type=jnp.float32)]
    pallas_call x0 -> x12, Pallas kernels: none -> 161 us  [the longest x2 37 us: attn_bwd(): pl.pallas_call(functools.partial(attn_bwd_kernel, causal, same), out_shap...]
    psum x0 -> x1, waiting for transfers between devices: none -> 113 us  [shards(): every = lax.psum(every, ('section', 'dp'))]
    unnamed x11 -> x4, waiting for transfers between devices: 59.3 us -> 0.55 us
    psum x1 -> x0, blocking collectives: 40.2 us -> none  [shards(): lax.psum((cross_bias_full, cross_part[8]), ('section', 'dp'))]
    unnamed x119 -> x47, local copies, waits for them, and re-layouts: 39 us -> 2.42 us
  transfers between devices with their start and end apart: 10 -> 9, of which waited for: 9 -> 5; matrix products, arithmetic and copies ran while one was open for 6% -> 10% of each run, Pallas kernels for 0% -> 9%
where the time goes in v1:
time: 615 us; the launch traced here: 608 us
  waiting for transfers between devices  345 us (56%)
  Pallas kernels  161 us (26%)
  local copies, waits for them, and re-layouts  48.1 us (8%)
  other arithmetic  20.3 us (3%)
  between operations  16.3 us (3%)
  loops' own time  9.94 us (2%)
  starting transfers between devices  7.85 us (1%)
    reduce_scatter x3, waiting for transfers between devices, scatter(): return lax.psum_scatter(value, 'dp', scatter_dimension=dim, tiled=True)  122 us
    psum x1, waiting for transfers between devices, shards(): every = lax.psum(every, ('section', 'dp'))  113 us
    ppermute x5, waiting for transfers between devices, send(): return lax.ppermute(value, 'section', [(0, 1)] if steps > 0 else [(1, 0)])  110 us
    pallas_call x2, Pallas kernels, attn_bwd(): pl.pallas_call(functools.partial(attn_bwd_kernel, causal, same), out_shap...  37 us
    pallas_call x2, Pallas kernels, ffn_fwd(): pl.pallas_call(functools.partial(ffn_fwd_kernel, chunk), out_shape=(jax.S...  32.5 us
    pallas_call x4, Pallas kernels, wgrad(): pl.pallas_call(functools.partial(wgrad_kernel, lengths), out_shape=jax.Sh...  31.2 us
    pallas_call x2, Pallas kernels, ffn_bwd(): pl.pallas_call(functools.partial(ffn_bwd_kernel, chunk, extra), out_shape...  30.4 us
    another operation x27, local copies, waits for them, and re-layouts  30.2 us
  transfers between devices with their start and end apart: 9, of which 5 were waited for; matrix products, arithmetic and copies ran while one was open for 10% of the time, Pallas kernels for 9%

profile of v1, /device:TPU:0, one launch (start us, length us, event | category | flops | bytes accessed | tf_op | source)
XLA Modules:
  0.0 608.0 jit_solution(17768589336840722341)
XLA Ops:
  10.1 40.6 %conditional.8 = (bf16[640,2304]{1,0:T(8,128)(2,1)}, bf16[640,768]{1,0:T(8,128)(2,1)}, f32[640,768]{1,0:T(8,128)}, f32[640,768]{1,0:T(8,128)}, f32[640,128]{1,0:...) conditional(s32[]{:T(128)} %convert_element_type.4, ...), branch_computations={%region_0.0_spmd, %region_1.0_spmd} | conditional | bytes 11141222 | solution.py:366
  10.1 19.7 %branch_0_fun.10 = (bf16[640,2304]{1,0:T(8,128)(2,1)}, bf16[640,768]{1,0:T(8,128)(2,1)}, f32[640,768]{1,0:T(8,128)}, f32[640,768]{1,0:T(8,128)}, f32[640,128]{1,0:T(8,128)}, /*index=5*/f32[640,768]{1,0:T(8,128)S(1)}) custom-call(s32[1,1]{1,0:T(1,128)} %get-tuple-element.293.len_ref, bf16[640,768]{1,0:T(8,128)(2,1)} %get-tuple-element.294.xq_ref.xkv_ref.res_ref, ...), custom_call_target="tpu_custom_call" | custom-call | tf_op jit(solution)/shard_map/cond/branch_0_fun/pallas_call | solution.py:95
  29.9 20.6 %branch_0_fun.11 = (bf16[640,768]{1,0:T(8,128)(2,1)}, bf16[640,3072]{1,0:T(8,128)(2,1)}, bf16[640,3072]{1,0:T(8,128)(2,1)}, f32[640,768]{1,0:T(8,128)}, f32[640,128]{1,0:T(8,128)S(1)}) custom-call(f32[640,768]{1,0:T(8,128)S(1)} %get-tuple-element.702.n_ref, bf16[768,3072]{1,0:T(8,128)(2,1)} %get-tuple-element.305.we_ref, ...), custom_call_target="tpu_custom_call" | custom-call | tf_op jit(solution)/shard_map/cond/branch_0_fun/pallas_call | solution.py:226
  53.6 21.9 %conditional.10 = (bf16[256,2304]{1,0:T(8,128)(2,1)}, bf16[256,768]{1,0:T(8,128)(2,1)}, f32[256,768]{1,0:T(8,128)}, f32[256,768]{1,0:T(8,128)}, f32[256,128]{1,0...) conditional(s32[]{:T(128)} %convert_element_type.4, ...), branch_computations={%region_4.0_spmd, %region_5.0_spmd} | conditional | bytes 4456550 | solution.py:366
  53.7 10.0 %branch_0_fun.12 = (bf16[256,2304]{1,0:T(8,128)(2,1)}, bf16[256,768]{1,0:T(8,128)(2,1)}, f32[256,768]{1,0:T(8,128)}, f32[256,768]{1,0:T(8,128)}, f32[256,128]{1,0:T(8,128)}, /*index=5*/f32[256,768]{1,0:T(8,128)S(1)}) custom-call(s32[1,1]{1,0:T(1,128)} %get-tuple-element.359.len_ref, bf16[256,768]{1,0:T(8,128)(2,1)S(1)} %get-tuple-element.360.xq_ref.xkv_ref.res_ref, ...), custom_call_target="tpu_custom_call" | custom-call | tf_op jit(solution)/shard_map/cond/branch_0_fun/pallas_call | solution.py:95
  63.7 11.8 %branch_0_fun.13 = (bf16[256,768]{1,0:T(8,128)(2,1)}, bf16[256,3072]{1,0:T(8,128)(2,1)}, bf16[256,3072]{1,0:T(8,128)(2,1)}, f32[256,768]{1,0:T(8,128)}, f32[256,128]{1,0:T(8,128)S(1)}) custom-call(f32[256,768]{1,0:T(8,128)S(1)} %get-tuple-element.750.n_ref, bf16[768,3072]{1,0:T(8,128)(2,1)} %get-tuple-element.371.we_ref, ...), custom_call_target="tpu_custom_call" | custom-call | tf_op jit(solution)/shard_map/cond/branch_0_fun/pallas_call | solution.py:226
  76.9 25.1 %conditional.9 = (f32[640,768]{1,0:T(8,128)}, bf16[640,3072]{1,0:T(8,128)(2,1)}, bf16[640,3072]{1,0:T(8,128)(2,1)}, bf16[640,768]{1,0:T(8,128)(2,1)}, bf16[640,7...) conditional(s32[]{:T(128)} %convert_element_type.4, () %tuple.73, ...), branch_computations={%region_2.0_spmd, %region_3.0_spmd} | conditional | bytes 19722380 | solution.py:398
  104.1 11.3 %conditional.11 = (f32[256,768]{1,0:T(8,128)}, bf16[256,3072]{1,0:T(8,128)(2,1)}, bf16[256,3072]{1,0:T(8,128)(2,1)}, bf16[256,768]{1,0:T(8,128)(2,1)}, bf16[256,...) conditional(s32[]{:T(128)} %convert_element_type.4, () %tuple.77, ...), branch_computations={%region_6.0_spmd, %region_7.0_spmd} | conditional | bytes 7925900 | solution.py:398
  116.7 108.1 %collective-permute-done.3 = bf16[256,768]{1,0:T(8,128)(2,1)S(1)} collective-permute-done((bf16[256,768]{1,0:T(8,128)(2,1)}, bf16[256,768]{1,0:T(8,128)(2,1)S(1)}, u32[]{:S(2)}, u32[]{:S(2)}) %collective-permute-start.3) | collective-permute-done | bytes 393248 | tf_op jit(solution)/shard_map/ppermute | solution.py:369
  224.8 23.7 %conditional.13 = (f32[256,768]{1,0:T(8,128)}, bf16[256,2304]{1,0:T(8,128)(2,1)}, bf16[256,768]{1,0:T(8,128)(2,1)}, f32[8,768]{1,0:T(8,128)}, bf16[256,3072]{1,0...) conditional(s32[]{:T(128)} %convert_element_type.4, ...), branch_computations={%region_10.0_spmd, %region_11.0_spmd} | conditional | bytes 3694768 | solution.py:415
  225.6 11.7 %branch_0_fun.16 = (f32[256,768]{1,0:T(8,128)}, bf16[256,3072]{1,0:T(8,128)(2,1)}, bf16[256,768]{1,0:T(8,128)(2,1)}, f32[8,768]{1,0:T(8,128)S(1)}, f32[1,3072]{1,0:T(1,128)S(1)}) custom-call(s32[1,1]{1,0:T(1,128)} %get-tuple-element.464.len_ref, bf16[256,768]{1,0:T(8,128)(2,1)} %get-tuple-element.465.cot_ref, bf16[256,768]{1,0:T(8,128)(2,1)} %copy-done.32, ...), custom_call_target="tpu_custom_call" | custom-call | tf_op jit(solution)/shard_map/cond/branch_0_fun/pallas_call | solution.py:270
  237.2 10.9 %branch_0_fun.17 = (f32[256,768]{1,0:T(8,128)}, bf16[256,2304]{1,0:T(8,128)(2,1)}, bf16[256,768]{1,0:T(8,128)(2,1)}, bf16[8,128]{1,0:T(8,128)(2,1)}, f32[8,768]{1,0:T(8,128)}) custom-call(s32[1,1]{1,0:T(1,128)} %get-tuple-element.464.len_ref, f32[256,768]{1,0:T(8,128)} %get-tuple-element.473.dn_ref, bf16[256,2304]{1,0:T(8,128)(2,1)} %get-tuple-element.474.qkv_ref, ...), custom_call_target="tpu_custom_call" | custom-call | tf_op jit(solution)/shard_map/cond/branch_0_fun/pallas_call | solution.py:184
  249.9 45.0 %conditional.12 = (f32[640,768]{1,0:T(8,128)}, bf16[640,2304]{1,0:T(8,128)(2,1)}, bf16[640,768]{1,0:T(8,128)(2,1)}, f32[8,768]{1,0:T(8,128)}, bf16[640,3072]{1,0...) conditional(s32[]{:T(128)} %convert_element_type.4, (s32[1,1]{1,0:T(1,128)}, ...), branch_computations={%region_8.0_spmd, %region_9.0_spmd} | conditional | bytes 4952140 | solution.py:415
  250.0 18.8 %branch_0_fun.14 = (f32[640,768]{1,0:T(8,128)}, bf16[640,3072]{1,0:T(8,128)(2,1)}, bf16[640,768]{1,0:T(8,128)(2,1)}, f32[8,768]{1,0:T(8,128)}, f32[1,3072]{1,0:T(1,128)}) custom-call(s32[1,1]{1,0:T(1,128)} %get-tuple-element.425.len_ref, bf16[640,768]{1,0:T(8,128)(2,1)} %get-tuple-element.426.cot_ref, bf16[640,768]{1,0:T(8,128)(2,1)} %get-tuple-element.427.dm_ref, ...), custom_call_target="tpu_custom_call" | custom-call | tf_op jit(solution)/shard_map/cond/branch_0_fun/pallas_call | solution.py:270
  268.8 26.1 %branch_0_fun.15 = (f32[640,768]{1,0:T(8,128)}, bf16[640,2304]{1,0:T(8,128)(2,1)}, bf16[640,768]{1,0:T(8,128)(2,1)}, bf16[8,128]{1,0:T(8,128)(2,1)}, f32[8,768]{1,0:T(8,128)}) custom-call(s32[1,1]{1,0:T(1,128)} %get-tuple-element.425.len_ref, f32[640,768]{1,0:T(8,128)} %get-tuple-element.434.dn_ref, bf16[640,2304]{1,0:T(8,128)(2,1)} %get-tuple-element.435.qkv_ref, ...), custom_call_target="tpu_custom_call" | custom-call | tf_op jit(solution)/shard_map/cond/branch_0_fun/pallas_call | solution.py:184
  295.0 19.9 %conditional.14 = (bf16[768,3072]{1,0:T(8,128)(2,1)}, bf16[3072,768]{1,0:T(8,128)(2,1)}, f32[8,768]{1,0:T(8,128)}, f32[8,768]{1,0:T(8,128)}, f32[1,3072]{1,0:T(1,128)}, /*index=5*/f32[1,3072]{1,0:T(1,128)}) conditional(s32[]{:T(128)} %convert_element_type.4, (f32[256,768]{1,0:T(8,128)}, f32[640,768]{1,0:T(8,128)}, bf16[256,3072]{1,0:T(8,128)(2,1)}, ...), branch_computations={%region_12.0_spmd, %region_13.0_spmd} | conditional | bytes 15728716 | solution.py:457
  295.1 9.9 %branch_0_fun.18 = bf16[768,3072]{1,0:T(8,128)(2,1)} custom-call(f32[256,768]{1,0:T(8,128)} %get-tuple-element.503.refs_0_, f32[640,768]{1,0:T(8,128)} %get-tuple-element.504.refs_1_, bf16[256,3072]{1,0:T(8,128)(2,1)} %get-tuple-element.505.refs_2_, bf16[640,3072]{1,0:T(8,128)(2,1)} %get-tuple-element.506.refs_3_), custom_call_target="tpu_custom_call" | custom-call | tf_op jit(solution)/shard_map/cond/branch_0_fun/pallas_call | solution.py:297
  305.0 9.8 %branch_0_fun.19 = bf16[3072,768]{1,0:T(8,128)(2,1)} custom-call(bf16[256,3072]{1,0:T(8,128)(2,1)} %get-tuple-element.507.refs_0_, bf16[640,3072]{1,0:T(8,128)(2,1)S(1)} %copy-done.12, bf16[256,768]{1,0:T(8,128)(2,1)} %get-tuple-element.509.refs_2_, bf16[640,768]{1,0:T(8,128)(2,1)} %get-tuple-element.510.refs_3_), custom_call_target="tpu_custom_call" | custom-call | tf_op jit(solution)/shard_map/cond/branch_0_fun/pallas_call | solution.py:297
  319.9 4.9 copy.34
  326.7 7.2 %shard_map.263 = bf16[768,2304]{1,0:T(8,128)(2,1)} custom-call(bf16[256,768]{1,0:T(8,128)(2,1)S(1)} %bitcast.77, bf16[640,768]{1,0:T(8,128)(2,1)S(1)} %bitcast.74, bf16[256,2304]{1,0:T(8,128)(2,1)S(1)} %copy-done.29, bf16[640,2304]{1,0:T(8,128)(2,1)} %get-tuple-element.650.refs_3_), custom_call_target="tpu_custom_call" | custom-call | tf_op jit(solution)/shard_map/pallas_call | solution.py:297
  338.1 8.1 %pad_maximum_fusion.1 = bf16[768,6144]{1,0:T(8,128)(2,1)} fusion(bf16[768,3072]{1,0:T(8,128)(2,1)} %get-tuple-element.675, bf16[768,768]{1,0:T(8,128)(2,1)} %shard_map.264, bf16[768,2304]{1,0:T(8,128)(2,1)S(1)} %copy-done.8), kind=kLoop, calls=%fused_computation.1 | loop fusion | flops 28311552 | bytes 18874368 | tf_op jit(solution)/shard_map/concatenate | solution.py:466
  349.3 112.6 %all-reduce.2.cloned.1.call-done = f32[29,768]{1,0:T(8,128)} async-done(((f32[29,768]{1,0:T(8,128)}), f32[29,768]{1,0:T(8,128)}) %all-reduce.2.cloned.1.call-update) | async-done | bytes 89104 | tf_op jit(solution)/shard_map/psum | solution.py:478
  473.1 9.4 %reduce-scatter.6.cloned.1.call-done = bf16[192,768]{1,0:T(8,128)(2,1)} async-done(((bf16[3072,768]{1,0:T(8,128)(2,1)}), bf16[192,768]{1,0:T(8,128)(2,1)}) %reduce-scatter.6.cloned.1.call-update) | async-done | bytes 294928 | tf_op jit(solution)/shard_map/reduce_scatter | solution.py:464
  484.3 112.4 %reduce-scatter.4.cloned.1.call-done = bf16[48,6144]{1,0:T(8,128)(2,1)} async-done(((bf16[768,6144]{1,0:T(8,128)(2,1)}), bf16[48,6144]{1,0:T(8,128)(2,1)}) %reduce-scatter.4.cloned.1.call-update) | async-done | bytes 589840 | tf_op jit(solution)/shard_map/reduce_scatter | solution.py:464
  (150 shorter events, 72.3 us)
Async XLA Ops:
  8.0 453.9 %all-reduce.2.cloned.1.call-start = ((), (), s32[]{:S(2)}) async-start(), calls=%async_computation.5 | async-start | bytes 196608 | tf_op jit(solution)/shard_map/psum | solution.py:478
  8.8 68.1 %copy-start.18 = (f32[1,6,768]{2,1,0:T(8,128)}, f32[1,6,768]{2,1,0:T(8,128)S(1)}, u32[]{:S(2)}) copy-start(f32[1,6,768]{2,1,0:T(8,128)S(1)} %copy.42) | copy-start | bytes 55300
  10.1 42.9 %copy-start.50 = (s32[2,1]{0,1:T(1,128)S(1)}, s32[2,1]{0,1:T(1,128)}, u32[]{:S(2)}) copy-start(s32[2,1]{0,1:T(1,128)} %param.37) | copy-start | bytes 28
  10.1 43.5 %copy-start.6 = (bf16[1,1,256,768]{3,2,1,0:T(8,128)(2,1)S(1)}, bf16[1,1,256,768]{3,2,1,0:T(8,128)(2,1)}, u32[]{:S(2)}) copy-start(bf16[1,1,256,768]{3,2,1,0:T(8,128)(2,1)} %param.33) | copy-start | bytes 1179652
  10.1 19.7 %copy-start.20 = (f32[2,768]{1,0:T(2,128)S(1)}, f32[2,768]{1,0:T(2,128)}, u32[]{:S(2)}) copy-start(f32[2,768]{1,0:T(2,128)} %get-tuple-element.298.gain_ref) | copy-start | bytes 18436 | tf_op jit(solution)/shard_map/cond
  10.1 19.7 %copy-start.34 = (f32[1,3072]{1,0:T(1,128)S(1)}, f32[1,3072]{1,0:T(1,128)}, u32[]{:S(2)}) copy-start(f32[1,3072]{1,0:T(1,128)} %get-tuple-element.307.be_ref) | copy-start | bytes 36868 | tf_op jit(solution)/shard_map/cond
  50.8 26.1 %copy-start.1 = (f32[640,768]{1,0:T(8,128)}, f32[640,768]{1,0:T(8,128)S(1)}, u32[]{:S(2)}) copy-start(f32[640,768]{1,0:T(8,128)S(1)} %get-tuple-element.621) | copy-start | bytes 5898244
  50.8 26.1 %collective-permute-start = (bf16[640,768]{1,0:T(8,128)(2,1)}, bf16[640,768]{1,0:T(8,128)(2,1)}, u32[]{:S(2)}, u32[]{:S(2)}) collective-permute-start(bf16[640,768]{1,0:T(8,128)(2,1)} %get-tuple-element.622), channel_id=1, source_target_pairs={{0,16},{1,17},{2,18},{3,19},{4,20},{5,21},{6,22},{7,23},{8,24},{9,... | collective-permute-start | bytes 2949128 | tf_op jit(solution)/shard_map/ppermute | solution.py:369
  53.6 23.2 %copy-start.49 = (f32[768]{0:T(1024)S(1)}, f32[768]{0:T(1024)}, u32[]{:S(2)}) copy-start(f32[768]{0:T(1024)} %param.47) | copy-start | bytes 9220
  53.6 23.3 %copy-start.44 = (f32[4,768]{1,0:T(4,128)S(1)}, f32[4,768]{1,0:T(4,128)}, u32[]{:S(2)}) copy-start(f32[4,768]{1,0:T(4,128)} %param.46) | copy-start | bytes 36868
  63.7 11.8 %copy-start.4 = (f32[256,768]{1,0:T(8,128)}, f32[256,768]{1,0:T(8,128)S(1)}, u32[]{:S(2)}) copy-start(f32[256,768]{1,0:T(8,128)S(1)} %get-tuple-element.750.n_ref) | copy-start | bytes 2359300 | tf_op jit(solution)/shard_map/cond
  75.5 27.9 %collective-permute-start.1 = (bf16[256,768]{1,0:T(8,128)(2,1)}, bf16[256,768]{1,0:T(8,128)(2,1)S(1)}, u32[]{:S(2)}, u32[]{:S(2)}) collective-permute-start(bf16[256,768]{1,0:T(8,128)(2,1)} %get-tuple-element.625), channel_id=1, source_target_pairs={{0,16},{1,17},{2,18},{3,19},{4,20},{5,21},{6,22},{7,23},{8,24},{9,... | collective-permute-start | bytes 1179656 | tf_op jit(solution)/shard_map/ppermute | solution.py:369
  102.1 147.9 %collective-permute-start.2 = (bf16[640,768]{1,0:T(8,128)(2,1)}, bf16[640,768]{1,0:T(8,128)(2,1)}, u32[]{:S(2)}, u32[]{:S(2)}) collective-permute-start(bf16[640,768]{1,0:T(8,128)(2,1)} %get-tuple-element.627), channel_id=1, source_target_pairs={{16,0},{17,1},{18,2},{19,3},{20,4},{21,5},{22,6},{23,7},{24,8},{25... | collective-permute-start | bytes 2949128 | tf_op jit(solution)/shard_map/ppermute | solution.py:369
  104.1 120.7 %copy-start = (bf16[1,768,2304]{2,1,0:T(8,128)(2,1)S(1)}, bf16[1,768,2304]{2,1,0:T(8,128)(2,1)}, u32[]{:S(2)}) copy-start(bf16[1,768,2304]{2,1,0:T(8,128)(2,1)} %param.38) | copy-start | bytes 10616836
  115.4 109.4 %collective-permute-start.3 = (bf16[256,768]{1,0:T(8,128)(2,1)}, bf16[256,768]{1,0:T(8,128)(2,1)S(1)}, u32[]{:S(2)}, u32[]{:S(2)}) collective-permute-start(bf16[256,768]{1,0:T(8,128)(2,1)} %get-tuple-element.638), channel_id=1, source_target_pairs={{16,0},{17,1},{18,2},{19,3},{20,4},{21,5},{22,6},{23,7},{24,8},{25... | collective-permute-start | bytes 1179656 | tf_op jit(solution)/shard_map/ppermute | solution.py:369
  250.0 18.8 %copy-start.25 = (f32[2,768]{1,0:T(2,128)S(1)}, f32[2,768]{1,0:T(2,128)}, u32[]{:S(2)}) copy-start(f32[2,768]{1,0:T(2,128)} %get-tuple-element.433.gain_ref) | copy-start | bytes 18436 | tf_op jit(solution)/shard_map/cond
  250.0 18.8 %copy-start.28 = (f32[640,128]{1,0:T(8,128)S(1)}, f32[640,128]{1,0:T(8,128)}, u32[]{:S(2)}) copy-start(f32[640,128]{1,0:T(8,128)} %get-tuple-element.439.r_ref) | copy-start | bytes 983044 | tf_op jit(solution)/shard_map/cond
  295.0 20.8 %copy-start.46 = (f32[8,768]{1,0:T(8,128)S(1)}, f32[8,768]{1,0:T(8,128)}, u32[]{:S(2)}) copy-start(f32[8,768]{1,0:T(8,128)} %get-tuple-element.677) | copy-start | bytes 73732
  295.0 20.8 %copy-start.47 = (f32[8,768]{1,0:T(8,128)S(1)}, f32[8,768]{1,0:T(8,128)}, u32[]{:S(2)}) copy-start(f32[8,768]{1,0:T(8,128)} %get-tuple-element.678) | copy-start | bytes 73732
  295.0 21.6 %copy-start.39 = (f32[5,768]{1,0:T(8,128)S(1)}, f32[5,768]{1,0:T(8,128)}, u32[]{:S(2)}) copy-start(f32[5,768]{1,0:T(8,128)} %slice_add_fusion) | copy-start | bytes 46084
  317.4 146.1 %reduce-scatter.8.cloned.1.call-start = ((), (), s32[]{:S(2)}) async-start(), calls=%async_computation.6 | async-start | bytes 5013504 | tf_op jit(solution)/shard_map/reduce_scatter | solution.py:464
  324.9 157.6 %reduce-scatter.6.cloned.1.call-start = ((), (), s32[]{:S(2)}) async-start(), calls=%async_computation.4 | async-start | bytes 5013504 | tf_op jit(solution)/shard_map/reduce_scatter | solution.py:464
  325.5 271.2 %reduce-scatter.4.cloned.1.call-start = ((), (), s32[]{:S(2)}) async-start(), calls=%async_computation.3 | async-start | bytes 10027008 | tf_op jit(solution)/shard_map/reduce_scatter | solution.py:464
  464.4 7.0 %collective-permute-start.4 = (bf16[96,768]{1,0:T(8,128)(2,1)S(1)}, bf16[96,768]{1,0:T(8,128)(2,1)S(1)}, u32[]{:S(2)}, u32[]{:S(2)}) collective-permute-start(bf16[96,768]{1,0:T(8,128)(2,1)S(1)} %slice.117), channel_id=1, source_target_pairs={{16,0},{17,1},{18,2},{19,3},{20,4},{21,5},{22,6},{23,7},{24,8},{25... | collective-permute-start | bytes 442376 | tf_op jit(solution)/shard_map/ppermute | solution.py:369
  (19 other events, 93.2 us)
Sparse Core Ops, SparseCore 0:
  317.5 144.3 all-reduce.1
Sparse Core Ops, SparseCore 1:
  325.0 79.1 reduce-scatter.7
  407.8 74.6 reduce-scatter.5
  486.4 110.2 reduce-scatter.3
